TPU v7x, 32 devices: a whole 2x2x4 slice. The times are simulated.
32 devices in a mesh: row: 4 (over z), col: 8 (over y, x, core).
Axes of the slice: x: 2, y: 2, z: 4, core: 2. Of those that a mesh axis runs over, the one named last changes fastest.
Arguments:
- slip_load: bfloat16 [4, 8, 1024, 128], P('row', 'col'), may hold values from -6 to 6
- flexibility: bfloat16 [4, 8, 1024, 1024], P('row', 'col'), as said below
- schur: bfloat16 [4, 8, 1024, 1024], P('row', 'col'), as said below
- corner_coupling: float32 [4, 8, 12, 1024], P('row', 'col'), may hold values from -0.1875 to 0.1875
- coarse_inverse: float32 [384, 384], P('row', 'col'), as said below
- bounds_table: float32 [16], replicated, may hold values from 0.3 to 3
- bound_index: int32 [4, 8, 1024], P('row', 'col'), may hold values from 0 to 15
- face_rows: int32 [4, 8, 4], P('row', 'col'), may hold values from 0 to 256, as said below
Outputs:
- multipliers: bfloat16 [4, 8, 1024, 128], P('row', 'col')
Inputs may be any that keep to these rules, and one draw needn't show every extreme that they name: `face_rows`: face counts agree between the two subdomains of a shared face, are 0 on faces at the edge of the grid, and some face has exactly 256 live slots. `coarse_inverse`: symmetric. `flexibility`: symmetric and positive definite. `schur`: symmetric and positive definite.
All inputs are finite; a program needn't handle non-finite values.
Results may differ from a plain program's by a relative error of at most 0.0038.
Values sent between devices are 32-bit elements; how exact they have to be, the bound alone decides.
No kernel may reach another device: no remote copies, remote signals or barrier semaphores. Data moves between devices by JAX's collectives and lax.ppermute only.
A program may use at most 64 MiB of HBM per device.

v0:
```python
import jax
import jax.numpy as jnp
from jax import lax
from jax.sharding import PartitionSpec as P

ITERS = 2


def passed_along(x, axis, by):
    count = lax.axis_size(axis)
    pairs = [(i, i + by) for i in range(count) if 0 <= i + by < count]
    return lax.ppermute(x, axis, pairs)


def broadcast(block, axis, holder):
    block = jnp.where(lax.axis_index(axis) == holder, block, jnp.zeros_like(block))
    return lax.psum(block, axis)


def local(
    slip_load,
    flexibility,
    schur,
    corner_coupling,
    coarse_inverse,
    bounds_table,
    bound_index,
    face_rows,
):
    loads = slip_load[0, 0].astype(jnp.float32)
    flex_block = flexibility[0, 0]
    schur_block = schur[0, 0]
    coupling = corner_coupling[0, 0]
    row_count = flex_block.shape[0]
    face_size = row_count // 4
    corners = coupling.shape[0]
    row_devices = lax.axis_size("row")
    row_index = lax.axis_index("row")
    col_index = lax.axis_index("col")
    levels = jnp.arange(bounds_table.shape[0], dtype=jnp.int32)
    onehot = (bound_index[0, 0][:, None] == levels[None, :]).astype(jnp.float32)
    bound = jnp.sum(onehot * bounds_table[None, :], axis=1)[:, None]
    slots = jnp.arange(face_size, dtype=jnp.int32)
    live = (slots[None, :] < face_rows[0, 0][:, None]).astype(jnp.float32).reshape(row_count, 1)
    lam = jnp.clip(loads, -bound, bound)
    for iteration in range(ITERS):
        displacement = jnp.dot(
            flex_block, lam.astype(jnp.bfloat16), preferred_element_type=jnp.float32
        )
        nb_west = passed_along(displacement[face_size : 2 * face_size], "col", 1)
        nb_east = passed_along(displacement[0:face_size], "col", -1)
        nb_lower = passed_along(displacement[3 * face_size :], "row", 1)
        nb_upper = passed_along(displacement[2 * face_size : 3 * face_size], "row", -1)
        paired = jnp.concatenate([nb_west, nb_east, nb_lower, nb_upper], axis=0)
        jump = live * (displacement - paired - loads)
        corner_force = jnp.dot(coupling, jump, precision=lax.Precision.HIGHEST)
        gathered = lax.all_gather(corner_force, "row", axis=0, tiled=True)
        partial_value = jnp.dot(coarse_inverse, gathered, precision=lax.Precision.HIGHEST)
        total = lax.psum(partial_value, "col")
        picked = broadcast(total, "row", col_index // 2)
        offset = col_index % 2 * (corners * row_devices) + row_index * corners
        coarse = lax.dynamic_slice_in_dim(picked, offset, corners, 0)
        correction = lax.dot_general(
            coupling, coarse, (((0,), (0,)), ((), ())), precision=lax.Precision.HIGHEST
        )
        projected = jump - correction
        projected_b = projected.astype(jnp.bfloat16)
        search = jnp.dot(schur_block, projected_b, preferred_element_type=jnp.float32)
        gain_local = jnp.sum(projected_b.astype(jnp.float32) * search, axis=0)
        search_b = search.astype(jnp.bfloat16)
        gain = lax.psum(gain_local, ("row", "col"))
        curved = jnp.dot(flex_block, search_b, preferred_element_type=jnp.float32)
        curvature = lax.psum(jnp.sum(search_b.astype(jnp.float32) * curved, axis=0), ("row", "col"))
        lam = jnp.clip(lam - (gain / curvature)[None, :] * search, -bound, bound)
    return lam.astype(jnp.bfloat16)[None, None]


def solution(mesh):
    return jax.shard_map(
        local,
        mesh=mesh,
        in_specs=(
            P("row", "col", None, None),
            P("row", "col", None, None),
            P("row", "col", None, None),
            P("row", "col", None, None),
            P("row", "col"),
            P(),
            P("row", "col", None),
            P("row", "col", None),
        ),
        out_specs=P("row", "col", None, None),
        check_vma=False,
    )
```

profile of v0, /device:TPU:14, one launch (start us, length us, event | category | flops | bytes accessed | tf_op | source)
XLA Modules:
  0.0 235.4 jit_solution(16768184671712670383)
XLA Ops:
  2.1 2.4 %fusion.14 = f32[1024,128]{0,1:T(8,128)S(1)} fusion(bf16[1,1,1024,1024]{3,2,1,0:T(8,128)(2,1)} %param.9, bf16[1,1,1024,128]{2,3,1,0:T(8,128)(2,1)S(1)} %copy.15, f32[1024]{0:T(1024)S(1)} %neg.10, f32[1024]{0:T(1024)S(1)} %select_reduce_fusion), kind=kOutput, calls=%fused_computation.16 | convolution fusion | flops 269221888 | bytes 2891776 | tf_op jit(solution)/shard_map/dot_general | solution.py:47
  5.3 1.9 collective-permute-start
  7.2 2.4 %collective-permute-start.3 = (f32[256,128]{0,1:T(8,128)}, f32[256,128]{0,1:T(8,128)S(1)}, u32[]{:S(2)}, u32[]{:S(2)}) collective-permute-start(f32[256,128]{0,1:T(8,128)} %get-tuple-element.14), channel_id=1, source_target_pairs={{8,0},{16,8},{24,16},{9,1},{17,9},{25,17},{10,2},{18,10},{26,18},{... | collective-permute-start | bytes 393224 | tf_op jit(solution)/shard_map/ppermute | solution.py:12
  9.6 3.5 %collective-permute-start.2 = (f32[256,128]{0,1:T(8,128)}, f32[256,128]{0,1:T(8,128)S(1)}, u32[]{:S(2)}, u32[]{:S(2)}) collective-permute-start(f32[256,128]{0,1:T(8,128)} %get-tuple-element.15), channel_id=1, source_target_pairs={{0,8},{8,16},{16,24},{1,9},{9,17},{17,25},{2,10},{10,18},{18,26},{... | collective-permute-start | bytes 393224 | tf_op jit(solution)/shard_map/ppermute | solution.py:12
  13.1 3.1 %collective-permute-start.1 = (f32[256,128]{0,1:T(8,128)S(1)}, f32[256,128]{0,1:T(8,128)}, u32[]{:S(2)}, u32[]{:S(2)}) collective-permute-start(f32[256,128]{0,1:T(8,128)S(1)} %get-tuple-element.16), channel_id=1, source_target_pairs={{1,0},{2,1},{3,2},{4,3},{5,4},{6,5},{7,6},{9,8},{10,9},{11,10},{12... | collective-permute-start | bytes 393224 | tf_op jit(solution)/shard_map/ppermute | solution.py:12
  16.6 2.0 collective-permute-done.1
  18.7 1.5 convolution_bitcast_fusion.5
  20.1 11.5 %all-gather = f32[4,12,128]{2,1,0:T(8,128)S(1)} all-gather(f32[1,12,128]{2,1,0:T(8,128)S(1)} %convolution_bitcast_fusion.5), channel_id=1, replica_groups=mesh['row'=4,'col'=8] {'row'}, dimensions={0}, use_global_device_ids=true | all-gather | bytes 30720 | tf_op jit(solution)/shard_map/all_gather | solution.py:57
  31.9 21.2 %psum.56 = f32[96,128]{1,0:T(8,128)S(1)} all-reduce(f32[96,128]{1,0:T(8,128)S(1)} %convolution_bitcast_fusion.3), channel_id=1, replica_groups=mesh['row'=4,'col'=8] {'col'}, use_global_device_ids=true, to_apply=%region_1.2 | all-reduce | flops 12288 | bytes 98304 | tf_op jit(solution)/shard_map/psum | solution.py:59
  53.1 16.4 %psum.57 = f32[96,128]{1,0:T(8,128)S(1)} all-reduce(f32[96,128]{1,0:T(8,128)S(1)} %broadcast_select_fusion.1), channel_id=1, replica_groups=mesh['row'=4,'col'=8] {'row'}, use_global_device_ids=true, to_apply=%region_2.3 | all-reduce | flops 12288 | bytes 98304 | tf_op jit(solution)/shard_map/psum | solution.py:17
  69.5 1.7 fusion.39
  73.0 44.6 %all-reduce.1 = (f32[128]{0:T(128)S(1)}, f32[128]{0:T(128)S(1)}) all-reduce(f32[128]{0:T(128)S(1)} %get-tuple-element.17, f32[128]{0:T(128)S(1)} %fusion.40), channel_id=1, replica_groups=mesh['row'=4,'col'=8] {'row','col'}, use_global_device_ids=true, to_apply=%region_4.5 | all-reduce | flops 256 | bytes 2048 | tf_op jit(solution)/shard_map/psum | solution.py:71
  117.7 2.4 %fusion.20 = f32[1024,128]{0,1:T(8,128)S(1)} fusion(bf16[1,1,1024,1024]{3,2,1,0:T(8,128)(2,1)} %param.9, bf16[1,1,1024,128]{2,3,1,0:T(8,128)(2,1)S(1)} %copy.15, f32[1024,128]{0,1:T(8,128)S(1)} %get-tuple-element.18, f32[128]{0:T(128)S(1)} %div.18, f32[1024]{0:T(1024)S(1)} %neg.10, f32[1024]{0:T(1024)S(1)} %select_reduce_fusion), kind=kOutput, calls=%fused_computation.18 | convolution fusion | flops 269484032 | bytes 3416576 | tf_op jit(solution)/shard_map/dot_general | solution.py:47
  120.2 1.9 collective-permute-start.4
  122.1 1.9 collective-permute-start.7
  124.0 3.9 %collective-permute-start.6 = (f32[256,128]{0,1:T(8,128)S(1)}, f32[256,128]{0,1:T(8,128)S(1)}, u32[]{:S(2)}, u32[]{:S(2)}) collective-permute-start(f32[256,128]{0,1:T(8,128)S(1)} %get-tuple-element.11), channel_id=1, source_target_pairs={{0,8},{8,16},{16,24},{1,9},{9,17},{17,25},{2,10},{10,18},{18,26},{... | collective-permute-start | bytes 393224 | tf_op jit(solution)/shard_map/ppermute | solution.py:12
  128.0 3.1 %collective-permute-start.5 = (f32[256,128]{0,1:T(8,128)S(1)}, f32[256,128]{0,1:T(8,128)S(1)}, u32[]{:S(2)}, u32[]{:S(2)}) collective-permute-start(f32[256,128]{0,1:T(8,128)S(1)} %get-tuple-element.12), channel_id=1, source_target_pairs={{1,0},{2,1},{3,2},{4,3},{5,4},{6,5},{7,6},{9,8},{10,9},{11,10},{12... | collective-permute-start | bytes 393224 | tf_op jit(solution)/shard_map/ppermute | solution.py:12
  131.1 2.4 %collective-permute-done.5 = f32[256,128]{0,1:T(8,128)S(1)} collective-permute-done((f32[256,128]{0,1:T(8,128)S(1)}, f32[256,128]{0,1:T(8,128)S(1)}, u32[]{:S(2)}, u32[]{:S(2)}) %collective-permute-start.5) | collective-permute-done | bytes 131104 | tf_op jit(solution)/shard_map/ppermute | solution.py:12
  134.2 11.3 %all-gather.1 = f32[4,12,128]{2,1,0:T(8,128)S(1)} all-gather(f32[1,12,128]{2,1,0:T(8,128)S(1)} %convolution_bitcast_fusion.4), channel_id=1, replica_groups=mesh['row'=4,'col'=8] {'row'}, dimensions={0}, use_global_device_ids=true | all-gather | bytes 30720 | tf_op jit(solution)/shard_map/all_gather | solution.py:57
  147.2 20.5 %psum.60 = f32[96,128]{1,0:T(8,128)S(1)} all-reduce(f32[96,128]{1,0:T(8,128)S(1)} %convolution_bitcast_fusion.2), channel_id=1, replica_groups=mesh['row'=4,'col'=8] {'col'}, use_global_device_ids=true, to_apply=%region_7.8 | all-reduce | flops 12288 | bytes 98304 | tf_op jit(solution)/shard_map/psum | solution.py:59
  167.7 16.3 %psum.61 = f32[96,128]{1,0:T(8,128)S(1)} all-reduce(f32[96,128]{1,0:T(8,128)S(1)} %broadcast_select_fusion), channel_id=1, replica_groups=mesh['row'=4,'col'=8] {'row'}, use_global_device_ids=true, to_apply=%region_8.9 | all-reduce | flops 12288 | bytes 98304 | tf_op jit(solution)/shard_map/psum | solution.py:17
  184.0 1.9 fusion.38
  187.8 44.8 %all-reduce = (f32[128]{0:T(128)S(1)}, f32[128]{0:T(128)S(1)}) all-reduce(f32[128]{0:T(128)S(1)} %get-tuple-element.19, f32[128]{0:T(128)S(1)} %fusion.43), channel_id=1, replica_groups=mesh['row'=4,'col'=8] {'row','col'}, use_global_device_ids=true, to_apply=%region_10.11 | all-reduce | flops 256 | bytes 2048 | tf_op jit(solution)/shard_map/psum | solution.py:71
  233.6 1.8 copy.16
  (61 shorter events, 10.5 us)
Async XLA Ops:
  0.0 71.2 %copy-start = (bf16[1,1,1024,1024]{3,2,1,0:T(8,128)(2,1)S(1)}, bf16[1,1,1024,1024]{3,2,1,0:T(8,128)(2,1)}, u32[]{:S(2)}) copy-start(bf16[1,1,1024,1024]{3,2,1,0:T(8,128)(2,1)} %param.10) | copy-start | bytes 6291460
  0.9 116.7 %copy-start.8 = (f32[1024]{0:T(1024)}, f32[1024]{0:T(1024)S(1)}, u32[]{:S(2)}) copy-start(f32[1024]{0:T(1024)S(1)} %select_reduce_fusion) | copy-start | bytes 12292
  1.0 116.7 %copy-start.11 = (f32[1024]{0:T(1024)}, f32[1024]{0:T(1024)S(1)}, u32[]{:S(2)}) copy-start(f32[1024]{0:T(1024)S(1)} %neg.10) | copy-start | bytes 12292
  2.1 14.1 %copy-start.16 = (s32[1,1,4]{2,1,0:T(1,128)S(1)}, s32[1,1,4]{2,1,0:T(1,128)}, u32[]{:S(2)}) copy-start(s32[1,1,4]{2,1,0:T(1,128)} %param.15) | copy-start | bytes 52
  2.1 16.6 %copy-start.3 = (f32[1,1,12,1024]{3,1,2,0:T(1,128)S(1)}, f32[1,1,12,1024]{3,1,2,0:T(1,128)}, u32[]{:S(2)}) copy-start(f32[1,1,12,1024]{3,1,2,0:T(1,128)} %param.11) | copy-start | bytes 147460
  2.1 29.5 %copy-start.10 = (f32[96,48]{0,1:T(8,128)S(1)}, f32[96,48]{0,1:T(8,128)}, u32[]{:S(2)}) copy-start(f32[96,48]{0,1:T(8,128)} %param.12) | copy-start | bytes 55300
  5.3 11.0 %collective-permute-start = (f32[256,128]{0,1:T(8,128)}, f32[256,128]{0,1:T(8,128)S(1)}, u32[]{:S(2)}, u32[]{:S(2)}) collective-permute-start(f32[256,128]{0,1:T(8,128)} %get-tuple-element.13), channel_id=1, source_target_pairs={{0,1},{1,2},{2,3},{3,4},{4,5},{5,6},{6,7},{8,9},{9,10},{10,11},{11... | collective-permute-start | bytes 393224 | tf_op jit(solution)/shard_map/ppermute | solution.py:12
  7.2 9.1 %collective-permute-start.3 = (f32[256,128]{0,1:T(8,128)}, f32[256,128]{0,1:T(8,128)S(1)}, u32[]{:S(2)}, u32[]{:S(2)}) collective-permute-start(f32[256,128]{0,1:T(8,128)} %get-tuple-element.14), channel_id=1, source_target_pairs={{8,0},{16,8},{24,16},{9,1},{17,9},{25,17},{10,2},{18,10},{26,18},{... | collective-permute-start | bytes 393224 | tf_op jit(solution)/shard_map/ppermute | solution.py:12
  9.6 7.1 %collective-permute-start.2 = (f32[256,128]{0,1:T(8,128)}, f32[256,128]{0,1:T(8,128)S(1)}, u32[]{:S(2)}, u32[]{:S(2)}) collective-permute-start(f32[256,128]{0,1:T(8,128)} %get-tuple-element.15), channel_id=1, source_target_pairs={{0,8},{8,16},{16,24},{1,9},{9,17},{17,25},{2,10},{10,18},{18,26},{... | collective-permute-start | bytes 393224 | tf_op jit(solution)/shard_map/ppermute | solution.py:12
  13.1 5.6 %collective-permute-start.1 = (f32[256,128]{0,1:T(8,128)S(1)}, f32[256,128]{0,1:T(8,128)}, u32[]{:S(2)}, u32[]{:S(2)}) collective-permute-start(f32[256,128]{0,1:T(8,128)S(1)} %get-tuple-element.16), channel_id=1, source_target_pairs={{1,0},{2,1},{3,2},{4,3},{5,4},{6,5},{7,6},{9,8},{10,9},{11,10},{12... | collective-permute-start | bytes 393224 | tf_op jit(solution)/shard_map/ppermute | solution.py:12
  16.3 117.3 %copy-start.13 = (f32[1,2,4,128]{3,1,2,0:T(2,128)}, f32[1,2,4,128]{3,1,2,0:T(2,128)S(1)}, u32[]{:S(2)}) copy-start(f32[1,2,4,128]{3,1,2,0:T(2,128)S(1)} %copy.18) | copy-start | bytes 12292
  69.5 2.6 %copy-start.1 = (bf16[1,1,1024,1024]{3,2,1,0:T(8,128)(2,1)S(1)}, bf16[1,1,1024,1024]{3,2,1,0:T(8,128)(2,1)}, u32[]{:S(2)}) copy-start(bf16[1,1,1024,1024]{3,2,1,0:T(8,128)(2,1)} %param.9) | copy-start | bytes 6291460
  117.7 2.5 %copy-start.14 = (f32[128]{0:T(128)}, f32[128]{0:T(128)S(1)}, u32[]{:S(2)}) copy-start(f32[128]{0:T(128)S(1)} %div.18) | copy-start | bytes 1540
  120.2 10.9 %collective-permute-start.4 = (f32[256,128]{0,1:T(8,128)S(1)}, f32[256,128]{0,1:T(8,128)S(1)}, u32[]{:S(2)}, u32[]{:S(2)}) collective-permute-start(f32[256,128]{0,1:T(8,128)S(1)} %get-tuple-element.9), channel_id=1, source_target_pairs={{0,1},{1,2},{2,3},{3,4},{4,5},{5,6},{6,7},{8,9},{9,10},{10,11},{11... | collective-permute-start | bytes 393224 | tf_op jit(solution)/shard_map/ppermute | solution.py:12
  122.1 9.0 %collective-permute-start.7 = (f32[256,128]{0,1:T(8,128)S(1)}, f32[256,128]{0,1:T(8,128)S(1)}, u32[]{:S(2)}, u32[]{:S(2)}) collective-permute-start(f32[256,128]{0,1:T(8,128)S(1)} %get-tuple-element.10), channel_id=1, source_target_pairs={{8,0},{16,8},{24,16},{9,1},{17,9},{25,17},{10,2},{18,10},{26,18},{... | collective-permute-start | bytes 393224 | tf_op jit(solution)/shard_map/ppermute | solution.py:12
  124.0 7.1 %collective-permute-start.6 = (f32[256,128]{0,1:T(8,128)S(1)}, f32[256,128]{0,1:T(8,128)S(1)}, u32[]{:S(2)}, u32[]{:S(2)}) collective-permute-start(f32[256,128]{0,1:T(8,128)S(1)} %get-tuple-element.11), channel_id=1, source_target_pairs={{0,8},{8,16},{16,24},{1,9},{9,17},{17,25},{2,10},{10,18},{18,26},{... | collective-permute-start | bytes 393224 | tf_op jit(solution)/shard_map/ppermute | solution.py:12
  128.0 5.6 %collective-permute-start.5 = (f32[256,128]{0,1:T(8,128)S(1)}, f32[256,128]{0,1:T(8,128)S(1)}, u32[]{:S(2)}, u32[]{:S(2)}) collective-permute-start(f32[256,128]{0,1:T(8,128)S(1)} %get-tuple-element.12), channel_id=1, source_target_pairs={{1,0},{2,1},{3,2},{4,3},{5,4},{6,5},{7,6},{9,8},{10,9},{11,10},{12... | collective-permute-start | bytes 393224 | tf_op jit(solution)/shard_map/ppermute | solution.py:12
  131.1 2.5 %copy-start.4 = (f32[256,128]{0,1:T(8,128)}, f32[256,128]{0,1:T(8,128)S(1)}, u32[]{:S(2)}) copy-start(f32[256,128]{0,1:T(8,128)S(1)} %collective-permute-done.4) | copy-start | bytes 393220
  131.1 3.0 %copy-start.5 = (f32[256,128]{0,1:T(8,128)}, f32[256,128]{0,1:T(8,128)S(1)}, u32[]{:S(2)}) copy-start(f32[256,128]{0,1:T(8,128)S(1)} %collective-permute-done.7) | copy-start | bytes 393220
  131.1 3.0 %copy-start.6 = (f32[256,128]{0,1:T(8,128)}, f32[256,128]{0,1:T(8,128)S(1)}, u32[]{:S(2)}) copy-start(f32[256,128]{0,1:T(8,128)S(1)} %collective-permute-done.6) | copy-start | bytes 393220
  184.0 2.9 %copy-start.2 = (bf16[1,1,1024,1024]{3,2,1,0:T(8,128)(2,1)S(1)}, bf16[1,1,1024,1024]{3,2,1,0:T(8,128)(2,1)}, u32[]{:S(2)}) copy-start(bf16[1,1,1024,1024]{3,2,1,0:T(8,128)(2,1)} %param.9) | copy-start | bytes 6291460
  185.9 46.7 %copy-start.9 = (f32[1024]{0:T(1024)S(1)}, f32[1024]{0:T(1024)}, u32[]{:S(2)}) copy-start(f32[1024]{0:T(1024)} %copy-done.8) | copy-start | bytes 12292
  185.9 46.7 %copy-start.12 = (f32[1024]{0:T(1024)S(1)}, f32[1024]{0:T(1024)}, u32[]{:S(2)}) copy-start(f32[1024]{0:T(1024)} %copy-done.11) | copy-start | bytes 12292
  185.9 46.6 %copy-start.15 = (f32[128]{0:T(128)S(1)}, f32[128]{0:T(128)}, u32[]{:S(2)}) copy-start(f32[128]{0:T(128)} %copy-done.14) | copy-start | bytes 1540
  (1 other events, 0.7 us)
where the time goes:
time: 236 us; the launch traced here: 235 us
  blocking collectives  187 us (79%)
  starting transfers between devices  21.7 us (9%)
  matrix products  15.4 us (7%)
  waiting for transfers between devices  4.82 us (2%)
  local copies, waits for them, and re-layouts  4.43 us (2%)
    psum x2, blocking collectives, local(): gain = lax.psum(gain_local, ('row', 'col'))  89.4 us
    psum x2, blocking collectives, local(): total = lax.psum(partial_value, 'col')  41.7 us
    psum x2, blocking collectives, broadcast(): return lax.psum(block, axis)  32.7 us
    all_gather x2, blocking collectives, local(): gathered = lax.all_gather(corner_force, 'row', axis=0, tiled=True)  22.8 us
    ppermute x8, starting transfers between devices, passed_along(): return lax.ppermute(x, axis, pairs)  21.7 us
    dot_general x2, matrix products, local(): jnp.dot(flex_block, lam.astype(jnp.bfloat16), preferred_element_type=jnp....  4.86 us
    ppermute x8, waiting for transfers between devices, passed_along(): return lax.ppermute(x, axis, pairs)  4.82 us
  transfers between devices with their start and end apart: 8, of which 3 were waited for; matrix products, arithmetic and copies ran while one was open for 0% of the time, Pallas kernels for 0%

commit v1 on v0

--- a/solution.py
+++ b/solution.py
@@ -68,7 +68,8 @@
         search = jnp.dot(schur_block, projected_b, preferred_element_type=jnp.float32)
         gain_local = jnp.sum(projected_b.astype(jnp.float32) * search, axis=0)
         search_b = search.astype(jnp.bfloat16)
-        gain = lax.psum(gain_local, ("row", "col"))
+        inner = lax.psum(gain_local, "col")
+        gain = lax.psum(inner, "row")
         curved = jnp.dot(flex_block, search_b, preferred_element_type=jnp.float32)
         curvature = lax.psum(jnp.sum(search_b.astype(jnp.float32) * curved, axis=0), ("row", "col"))
         lam = jnp.clip(lam - (gain / curvature)[None, :] * search, -bound, bound)

time: 236 us -> 282 us (1.19)
  blocking collectives: 187 us -> 229 us
  matrix products: 15.4 us -> 18.3 us
    psum x2 -> x6, blocking collectives: 89.4 us -> 130 us  [the longest x2 84.4 us: local(): lax.psum(jnp.sum(search_b.astype(jnp.float32) * curved, axis=0), ('row',...]
    dot_general x2, matrix products: 1.85 us -> 5 us  [local(): curved = jnp.dot(flex_block, search_b, preferred_element_type=jnp.float32)]
  transfers between devices with their start and end apart: 8 -> 8, of which waited for: 3 -> 4; matrix products, arithmetic and copies ran while one was open for 0% -> 0% of each run, Pallas kernels for 0% -> 0%
where the time goes in v1:
time: 282 us; the launch traced here: 280 us
  blocking collectives  229 us (81%)
  starting transfers between devices  21.7 us (8%)
  matrix products  18.3 us (6%)
  waiting for transfers between devices  4.83 us (2%)
  local copies, waits for them, and re-layouts  4.42 us (2%)
    psum x2, blocking collectives, local(): lax.psum(jnp.sum(search_b.astype(jnp.float32) * curved, axis=0), ('row',...  84.4 us
    psum x2, blocking collectives, local(): total = lax.psum(partial_value, 'col')  41.6 us
    psum x2, blocking collectives, broadcast(): return lax.psum(block, axis)  34 us
    psum x2, blocking collectives, local(): inner = lax.psum(gain_local, 'col')  23.8 us
    all_gather x2, blocking collectives, local(): gathered = lax.all_gather(corner_force, 'row', axis=0, tiled=True)  22.8 us
    psum x2, blocking collectives, local(): gain = lax.psum(inner, 'row')  22.3 us
    ppermute x8, starting transfers between devices, passed_along(): return lax.ppermute(x, axis, pairs)  21.7 us
  transfers between devices with their start and end apart: 8, of which 4 were waited for; matrix products, arithmetic and copies ran while one was open for 0% of the time, Pallas kernels for 0%

profile of v1, /device:TPU:14, one launch (start us, length us, event | category | flops | bytes accessed | tf_op | source)
XLA Modules:
  0.0 280.4 jit_solution(7773075990904049246)
XLA Ops:
  2.1 2.4 fusion.14
  7.2 2.4 collective-permute-start.3
  9.6 3.5 %collective-permute-start.2 = (f32[256,128]{0,1:T(8,128)}, f32[256,128]{0,1:T(8,128)S(1)}, u32[]{:S(2)}, u32[]{:S(2)}) collective-permute-start(f32[256,128]{0,1:T(8,128)} %get-tuple-element.11), channel_id=1, source_target_pairs={{0,8},{8,16},{16,24},{1,9},{9,17},{17,25},{2,10},{10,18},{18,26},{... | collective-permute-start | bytes 393224 | tf_op jit(solution)/shard_map/ppermute | solution.py:12
  13.1 3.1 %collective-permute-start.1 = (f32[256,128]{0,1:T(8,128)S(1)}, f32[256,128]{0,1:T(8,128)}, u32[]{:S(2)}, u32[]{:S(2)}) collective-permute-start(f32[256,128]{0,1:T(8,128)S(1)} %get-tuple-element.12), channel_id=1, source_target_pairs={{1,0},{2,1},{3,2},{4,3},{5,4},{6,5},{7,6},{9,8},{10,9},{11,10},{12... | collective-permute-start | bytes 393224 | tf_op jit(solution)/shard_map/ppermute | solution.py:12
  16.6 2.0 collective-permute-done.1
  20.1 11.5 %all-gather = f32[4,12,128]{2,1,0:T(8,128)S(1)} all-gather(f32[1,12,128]{2,1,0:T(8,128)S(1)} %convolution_bitcast_fusion.5), channel_id=1, replica_groups=mesh['row'=4,'col'=8] {'row'}, dimensions={0}, use_global_device_ids=true | all-gather | bytes 30720 | tf_op jit(solution)/shard_map/all_gather | solution.py:57
  31.9 21.2 %psum.70 = f32[96,128]{1,0:T(8,128)S(1)} all-reduce(f32[96,128]{1,0:T(8,128)S(1)} %convolution_bitcast_fusion.3), channel_id=1, replica_groups=mesh['row'=4,'col'=8] {'col'}, use_global_device_ids=true, to_apply=%region_1.2 | all-reduce | flops 12288 | bytes 98304 | tf_op jit(solution)/shard_map/psum | solution.py:59
  53.1 16.4 %psum.71 = f32[96,128]{1,0:T(8,128)S(1)} all-reduce(f32[96,128]{1,0:T(8,128)S(1)} %broadcast_select_fusion.1), channel_id=1, replica_groups=mesh['row'=4,'col'=8] {'row'}, use_global_device_ids=true, to_apply=%region_2.3 | all-reduce | flops 12288 | bytes 98304 | tf_op jit(solution)/shard_map/psum | solution.py:17
  71.9 11.9 %psum.72 = f32[128]{0:T(128)S(1)} all-reduce(f32[128]{0:T(128)S(1)} %get-tuple-element.13), channel_id=1, replica_groups=mesh['row'=4,'col'=8] {'col'}, use_global_device_ids=true, to_apply=%region_4.5 | all-reduce | flops 128 | bytes 1024 | tf_op jit(solution)/shard_map/psum | solution.py:71
  83.9 11.7 %psum.73 = f32[128]{0:T(128)S(1)} all-reduce(f32[128]{0:T(128)S(1)} %psum.72), channel_id=1, replica_groups=mesh['row'=4,'col'=8] {'row'}, use_global_device_ids=true, to_apply=%region_5.6 | all-reduce | flops 128 | bytes 1024 | tf_op jit(solution)/shard_map/psum | solution.py:72
  95.5 2.5 fusion.40
  98.0 41.7 %psum.74 = f32[128]{0:T(128)S(1)} all-reduce(f32[128]{0:T(128)S(1)} %fusion.40), channel_id=1, replica_groups=mesh['row'=4,'col'=8] {'row','col'}, use_global_device_ids=true, to_apply=%region_7.8 | all-reduce | flops 128 | bytes 1024 | tf_op jit(solution)/shard_map/psum | solution.py:74
  139.7 2.4 fusion.20
  142.2 1.9 collective-permute-start.4
  144.1 3.4 %collective-permute-start.7 = (f32[256,128]{0,1:T(8,128)S(1)}, f32[256,128]{0,1:T(8,128)S(1)}, u32[]{:S(2)}, u32[]{:S(2)}) collective-permute-start(f32[256,128]{0,1:T(8,128)S(1)} %get-tuple-element.6), channel_id=1, source_target_pairs={{8,0},{16,8},{24,16},{9,1},{17,9},{25,17},{10,2},{18,10},{26,18},{... | collective-permute-start | bytes 393224 | tf_op jit(solution)/shard_map/ppermute | solution.py:12
  147.5 2.5 collective-permute-start.6
  150.0 3.1 %collective-permute-start.5 = (f32[256,128]{0,1:T(8,128)S(1)}, f32[256,128]{0,1:T(8,128)S(1)}, u32[]{:S(2)}, u32[]{:S(2)}) collective-permute-start(f32[256,128]{0,1:T(8,128)S(1)} %get-tuple-element.8), channel_id=1, source_target_pairs={{1,0},{2,1},{3,2},{4,3},{5,4},{6,5},{7,6},{9,8},{10,9},{11,10},{12... | collective-permute-start | bytes 393224 | tf_op jit(solution)/shard_map/ppermute | solution.py:12
  156.3 11.4 %all-gather.1 = f32[4,12,128]{2,1,0:T(8,128)S(1)} all-gather(f32[1,12,128]{2,1,0:T(8,128)S(1)} %convolution_bitcast_fusion.4), channel_id=1, replica_groups=mesh['row'=4,'col'=8] {'row'}, dimensions={0}, use_global_device_ids=true | all-gather | bytes 30720 | tf_op jit(solution)/shard_map/all_gather | solution.py:57
  169.2 20.4 %psum.75 = f32[96,128]{1,0:T(8,128)S(1)} all-reduce(f32[96,128]{1,0:T(8,128)S(1)} %convolution_bitcast_fusion.2), channel_id=1, replica_groups=mesh['row'=4,'col'=8] {'col'}, use_global_device_ids=true, to_apply=%region_8.9 | all-reduce | flops 12288 | bytes 98304 | tf_op jit(solution)/shard_map/psum | solution.py:59
  189.7 17.6 %psum.76 = f32[96,128]{1,0:T(8,128)S(1)} all-reduce(f32[96,128]{1,0:T(8,128)S(1)} %broadcast_select_fusion), channel_id=1, replica_groups=mesh['row'=4,'col'=8] {'row'}, use_global_device_ids=true, to_apply=%region_9.10 | all-reduce | flops 12288 | bytes 98304 | tf_op jit(solution)/shard_map/psum | solution.py:17
  209.9 11.8 %psum.77 = f32[128]{0:T(128)S(1)} all-reduce(f32[128]{0:T(128)S(1)} %get-tuple-element.15), channel_id=1, replica_groups=mesh['row'=4,'col'=8] {'col'}, use_global_device_ids=true, to_apply=%region_11.12 | all-reduce | flops 128 | bytes 1024 | tf_op jit(solution)/shard_map/psum | solution.py:71
  221.8 10.7 %psum.78 = f32[128]{0:T(128)S(1)} all-reduce(f32[128]{0:T(128)S(1)} %psum.77), channel_id=1, replica_groups=mesh['row'=4,'col'=8] {'row'}, use_global_device_ids=true, to_apply=%region_12.13 | all-reduce | flops 128 | bytes 1024 | tf_op jit(solution)/shard_map/psum | solution.py:72
  232.4 2.5 fusion.43
  234.9 42.7 %psum.79 = f32[128]{0:T(128)S(1)} all-reduce(f32[128]{0:T(128)S(1)} %fusion.43), channel_id=1, replica_groups=mesh['row'=4,'col'=8] {'row','col'}, use_global_device_ids=true, to_apply=%region_14.15 | all-reduce | flops 128 | bytes 1024 | tf_op jit(solution)/shard_map/psum | solution.py:74
  (61 shorter events, 19.6 us)
Async XLA Ops:
  0.0 71.0 %copy-start = (bf16[1,1,1024,1024]{3,2,1,0:T(8,128)(2,1)S(1)}, bf16[1,1,1024,1024]{3,2,1,0:T(8,128)(2,1)}, u32[]{:S(2)}) copy-start(bf16[1,1,1024,1024]{3,2,1,0:T(8,128)(2,1)} %param.10) | copy-start | bytes 6291460
  0.9 138.8 %copy-start.6 = (f32[1024]{0:T(1024)}, f32[1024]{0:T(1024)S(1)}, u32[]{:S(2)}) copy-start(f32[1024]{0:T(1024)S(1)} %select_reduce_fusion) | copy-start | bytes 12292
  1.0 138.8 %copy-start.9 = (f32[1024]{0:T(1024)}, f32[1024]{0:T(1024)S(1)}, u32[]{:S(2)}) copy-start(f32[1024]{0:T(1024)S(1)} %neg.10) | copy-start | bytes 12292
  2.1 14.1 %copy-start.14 = (s32[1,1,4]{2,1,0:T(1,128)S(1)}, s32[1,1,4]{2,1,0:T(1,128)}, u32[]{:S(2)}) copy-start(s32[1,1,4]{2,1,0:T(1,128)} %param.15) | copy-start | bytes 52
  2.1 16.6 %copy-start.1 = (f32[1,1,12,1024]{3,1,2,0:T(1,128)S(1)}, f32[1,1,12,1024]{3,1,2,0:T(1,128)}, u32[]{:S(2)}) copy-start(f32[1,1,12,1024]{3,1,2,0:T(1,128)} %param.11) | copy-start | bytes 147460
  2.1 29.5 %copy-start.8 = (f32[96,48]{0,1:T(8,128)S(1)}, f32[96,48]{0,1:T(8,128)}, u32[]{:S(2)}) copy-start(f32[96,48]{0,1:T(8,128)} %param.12) | copy-start | bytes 55300
  5.3 11.0 %collective-permute-start = (f32[256,128]{0,1:T(8,128)}, f32[256,128]{0,1:T(8,128)S(1)}, u32[]{:S(2)}, u32[]{:S(2)}) collective-permute-start(f32[256,128]{0,1:T(8,128)} %get-tuple-element.9), channel_id=1, source_target_pairs={{0,1},{1,2},{2,3},{3,4},{4,5},{5,6},{6,7},{8,9},{9,10},{10,11},{11... | collective-permute-start | bytes 393224 | tf_op jit(solution)/shard_map/ppermute | solution.py:12
  7.2 9.1 %collective-permute-start.3 = (f32[256,128]{0,1:T(8,128)}, f32[256,128]{0,1:T(8,128)S(1)}, u32[]{:S(2)}, u32[]{:S(2)}) collective-permute-start(f32[256,128]{0,1:T(8,128)} %get-tuple-element.10), channel_id=1, source_target_pairs={{8,0},{16,8},{24,16},{9,1},{17,9},{25,17},{10,2},{18,10},{26,18},{... | collective-permute-start | bytes 393224 | tf_op jit(solution)/shard_map/ppermute | solution.py:12
  9.6 7.1 %collective-permute-start.2 = (f32[256,128]{0,1:T(8,128)}, f32[256,128]{0,1:T(8,128)S(1)}, u32[]{:S(2)}, u32[]{:S(2)}) collective-permute-start(f32[256,128]{0,1:T(8,128)} %get-tuple-element.11), channel_id=1, source_target_pairs={{0,8},{8,16},{16,24},{1,9},{9,17},{17,25},{2,10},{10,18},{18,26},{... | collective-permute-start | bytes 393224 | tf_op jit(solution)/shard_map/ppermute | solution.py:12
  13.1 5.6 %collective-permute-start.1 = (f32[256,128]{0,1:T(8,128)S(1)}, f32[256,128]{0,1:T(8,128)}, u32[]{:S(2)}, u32[]{:S(2)}) collective-permute-start(f32[256,128]{0,1:T(8,128)S(1)} %get-tuple-element.12), channel_id=1, source_target_pairs={{1,0},{2,1},{3,2},{4,3},{5,4},{6,5},{7,6},{9,8},{10,9},{11,10},{12... | collective-permute-start | bytes 393224 | tf_op jit(solution)/shard_map/ppermute | solution.py:12
  16.3 139.3 %copy-start.11 = (f32[1,2,4,128]{3,1,2,0:T(2,128)}, f32[1,2,4,128]{3,1,2,0:T(2,128)S(1)}, u32[]{:S(2)}) copy-start(f32[1,2,4,128]{3,1,2,0:T(2,128)S(1)} %copy.18) | copy-start | bytes 12292
  139.7 2.5 copy-start.12
  142.2 10.9 %collective-permute-start.4 = (f32[256,128]{0,1:T(8,128)S(1)}, f32[256,128]{0,1:T(8,128)S(1)}, u32[]{:S(2)}, u32[]{:S(2)}) collective-permute-start(f32[256,128]{0,1:T(8,128)S(1)} %get-tuple-element.5), channel_id=1, source_target_pairs={{0,1},{1,2},{2,3},{3,4},{4,5},{5,6},{6,7},{8,9},{9,10},{10,11},{11... | collective-permute-start | bytes 393224 | tf_op jit(solution)/shard_map/ppermute | solution.py:12
  144.1 9.0 %collective-permute-start.7 = (f32[256,128]{0,1:T(8,128)S(1)}, f32[256,128]{0,1:T(8,128)S(1)}, u32[]{:S(2)}, u32[]{:S(2)}) collective-permute-start(f32[256,128]{0,1:T(8,128)S(1)} %get-tuple-element.6), channel_id=1, source_target_pairs={{8,0},{16,8},{24,16},{9,1},{17,9},{25,17},{10,2},{18,10},{26,18},{... | collective-permute-start | bytes 393224 | tf_op jit(solution)/shard_map/ppermute | solution.py:12
  147.5 6.9 %collective-permute-start.6 = (f32[256,128]{0,1:T(8,128)S(1)}, f32[256,128]{0,1:T(8,128)S(1)}, u32[]{:S(2)}, u32[]{:S(2)}) collective-permute-start(f32[256,128]{0,1:T(8,128)S(1)} %get-tuple-element.7), channel_id=1, source_target_pairs={{0,8},{8,16},{16,24},{1,9},{9,17},{17,25},{2,10},{10,18},{18,26},{... | collective-permute-start | bytes 393224 | tf_op jit(solution)/shard_map/ppermute | solution.py:12
  150.0 5.6 %collective-permute-start.5 = (f32[256,128]{0,1:T(8,128)S(1)}, f32[256,128]{0,1:T(8,128)S(1)}, u32[]{:S(2)}, u32[]{:S(2)}) collective-permute-start(f32[256,128]{0,1:T(8,128)S(1)} %get-tuple-element.8), channel_id=1, source_target_pairs={{1,0},{2,1},{3,2},{4,3},{5,4},{6,5},{7,6},{9,8},{10,9},{11,10},{12... | collective-permute-start | bytes 393224 | tf_op jit(solution)/shard_map/ppermute | solution.py:12
  153.1 2.5 copy-start.2
  153.1 3.0 %copy-start.3 = (f32[256,128]{0,1:T(8,128)}, f32[256,128]{0,1:T(8,128)S(1)}, u32[]{:S(2)}) copy-start(f32[256,128]{0,1:T(8,128)S(1)} %collective-permute-done.7) | copy-start | bytes 393220
  154.4 1.8 copy-start.4
  155.6 0.7 copy-start.5
  209.0 68.6 %copy-start.7 = (f32[1024]{0:T(1024)S(1)}, f32[1024]{0:T(1024)}, u32[]{:S(2)}) copy-start(f32[1024]{0:T(1024)} %copy-done.6) | copy-start | bytes 12292
  209.0 68.6 %copy-start.10 = (f32[1024]{0:T(1024)S(1)}, f32[1024]{0:T(1024)}, u32[]{:S(2)}) copy-start(f32[1024]{0:T(1024)} %copy-done.9) | copy-start | bytes 12292
  209.0 68.6 %copy-start.13 = (f32[128]{0:T(128)S(1)}, f32[128]{0:T(128)}, u32[]{:S(2)}) copy-start(f32[128]{0:T(128)} %copy-done.12) | copy-start | bytes 1540
